TPU v7x, 32 devices: a whole 2x2x4 slice. The times are simulated.
32 devices in a mesh: lon: 8 (over z, y), lat: 4 (over x, core).
Axes of the slice: x: 2, y: 2, z: 4, core: 2. Of those that a mesh axis runs over, the one named last changes fastest.
Arguments:
- zonal_wind: float32 [8, 128, 1024], P(None, 'lat', 'lon'), may hold values from -6 to 6
- meridional_wind: float32 [8, 128, 1024], P(None, 'lat', 'lon'), may hold values from -6 to 6
- theta_field: float32 [8, 128, 1024], P(None, 'lat', 'lon'), may hold values from -6 to 6
- pressure: float32 [8, 128, 1024], P(None, 'lat', 'lon'), may hold values from -6 to 6
- stiffness: float32 [8, 128, 1024], P(None, 'lat', 'lon'), may hold values from 1 to 8
Outputs:
- zonal_next: float32 [8, 128, 1024], P(None, 'lat', 'lon')
- meridional_next: float32 [8, 128, 1024], P(None, 'lat', 'lon')
- theta_next: float32 [8, 128, 1024], P(None, 'lat', 'lon')
- pressure_next: float32 [8, 128, 1024], P(None, 'lat', 'lon')
All inputs are finite; a program needn't handle non-finite values.
Results may differ from a plain program's by a relative error of at most 0.00002.
Values sent between devices are 32-bit elements; how exact they have to be, the bound alone decides.
A program may use at most 64 MiB of HBM per device.

v0:
```python
import jax
import jax.numpy as jnp
from jax import lax
from jax.sharding import PartitionSpec as P

SWEEPS = 3


divergence_weight = 0.5
thermal_weight = 0.3
vertical_coupling = 0.5
gradient_weight = 0.5
adjust_weight = 0.5


def with_halo(cells, sides, width):
    for axis, dim in sides:
        count = lax.axis_size(axis)
        head = lax.slice_in_dim(cells, 0, width, axis=dim)
        tail = lax.slice_in_dim(cells, cells.shape[dim] - width, cells.shape[dim], axis=dim)
        cells = jnp.concatenate(
            [
                lax.ppermute(tail, axis, [(i, (i + 1) % count) for i in range(count)]),
                cells,
                lax.ppermute(head, axis, [((i + 1) % count, i) for i in range(count)]),
            ],
            axis=dim,
        )
    return cells


def passed_along(block, axis, distance):
    devices = range(lax.axis_size(axis))
    route = [((i - distance) % len(devices), i) for i in devices]
    return lax.ppermute(block, axis, route)


def extend(stacked, sign_list, margin):
    padded = with_halo(stacked, (("lon", 3), ("lat", 2)), margin)
    edge_rows = jnp.concatenate(
        [padded[:, :, margin : 2 * margin], padded[:, :, -2 * margin : -margin]], axis=2
    )
    antipodal = passed_along(edge_rows, "lon", lax.axis_size("lon") // 2)
    sign_array = jnp.asarray(sign_list, jnp.float32)[:, None, None, None]
    south_rows = sign_array * antipodal[:, :, :margin][:, :, ::-1]
    north_rows = sign_array * antipodal[:, :, margin:][:, :, ::-1]
    strip_index = lax.axis_index("lat")
    strip_count = lax.axis_size("lat")
    lower_rim = jnp.where(strip_index == 0, south_rows, padded[:, :, :margin])
    upper_rim = jnp.where(strip_index == strip_count - 1, north_rows, padded[:, :, -margin:])
    return jnp.concatenate([lower_rim, padded[:, :, margin:-margin], upper_rim], axis=2)


def make_source(zonal_ext, meridional_ext, pressure, theta_field):
    divergence = 0.5 * (zonal_ext[:, 1:-1, 2:] - zonal_ext[:, 1:-1, :-2]) + 0.5 * (
        meridional_ext[:, 2:, 1:-1] - meridional_ext[:, :-2, 1:-1]
    )
    return pressure - divergence_weight * divergence + thermal_weight * theta_field


def jacobi(iterate, stiff_ext, source_core):
    levels = iterate.shape[0]
    level_index = jnp.arange(levels)
    vertical = vertical_coupling * (
        (level_index > 0).astype(jnp.float32) + (level_index < levels - 1).astype(jnp.float32)
    )
    vertical = vertical[:, None, None]
    center = stiff_ext[:, 1:-1, 1:-1]
    east_face = 0.5 * (center + stiff_ext[:, 1:-1, 2:])
    west_face = 0.5 * (center + stiff_ext[:, 1:-1, :-2])
    north_face = 0.5 * (center + stiff_ext[:, 2:, 1:-1])
    south_face = 0.5 * (center + stiff_ext[:, :-2, 1:-1])
    center_value = iterate[:, 1:-1, 1:-1]
    above_level = jnp.concatenate([center_value[1:], jnp.zeros_like(center_value[:1])], axis=0)
    below_level = jnp.concatenate([jnp.zeros_like(center_value[:1]), center_value[:-1]], axis=0)
    numerator = source_core + east_face * iterate[:, 1:-1, 2:] + west_face * iterate[:, 1:-1, :-2]
    numerator = numerator + north_face * iterate[:, 2:, 1:-1] + south_face * iterate[:, :-2, 1:-1]
    numerator = numerator + vertical_coupling * (above_level + below_level)
    denominator = 1.0 + east_face + west_face + north_face + south_face + vertical
    return numerator / denominator


def shrinking_sweeps(source_wide, stiff_wide, rows_core, cols_core, margin):
    iterate = source_wide
    for sweep_index in range(SWEEPS):
        reach = margin - sweep_index
        stiff_part = stiff_wide[
            :,
            sweep_index : sweep_index + rows_core + 2 * reach,
            sweep_index : sweep_index + cols_core + 2 * reach,
        ]
        inner = sweep_index + 1
        source_part = source_wide[
            :,
            inner : inner + rows_core + 2 * (reach - 1),
            inner : inner + cols_core + 2 * (reach - 1),
        ]
        iterate = jacobi(iterate, stiff_part, source_part)
    return iterate


def on_device(zonal_wind, meridional_wind, theta_field, pressure, stiffness):
    rows_core = pressure.shape[1]
    cols_core = pressure.shape[2]
    winds = extend(jnp.stack([zonal_wind, meridional_wind]), [-1.0, -1.0], 1)
    source = make_source(winds[0], winds[1], pressure, theta_field)
    wide = extend(jnp.stack([source, stiffness]), [1.0, 1.0], SWEEPS + 1)
    final_ext = shrinking_sweeps(wide[0], wide[1], rows_core, cols_core, SWEEPS + 1)
    iterate = final_ext[:, 1:-1, 1:-1]
    east_west = 0.5 * (final_ext[:, 1:-1, 2:] - final_ext[:, 1:-1, :-2])
    north_south = 0.5 * (final_ext[:, 2:, 1:-1] - final_ext[:, :-2, 1:-1])
    zonal_next = zonal_wind - gradient_weight * east_west
    meridional_next = meridional_wind - gradient_weight * north_south
    theta_next = theta_field - adjust_weight * (iterate - pressure)
    return (zonal_next, meridional_next, theta_next, iterate)


def solution(mesh):
    return jax.shard_map(
        on_device,
        mesh=mesh,
        in_specs=(
            P(None, "lat", "lon"),
            P(None, "lat", "lon"),
            P(None, "lat", "lon"),
            P(None, "lat", "lon"),
            P(None, "lat", "lon"),
        ),
        out_specs=(
            P(None, "lat", "lon"),
            P(None, "lat", "lon"),
            P(None, "lat", "lon"),
            P(None, "lat", "lon"),
        ),
        check_vma=False,
    )
```

profile of v0, /device:TPU:0, one launch (start us, length us, event | category | flops | bytes accessed | tf_op | source)
XLA Modules:
  0.0 56.5 jit_solution(5775614177200635552)
XLA Ops:
  0.6 0.0 copy-start
  0.6 0.0 copy-start.1
  0.7 1.3 %slice_maximum_fusion.1 = (f32[2,8,32,1]{3,2,1,0:T(8,128)S(1)}, f32[2,8,32,1]{3,2,1,0:T(8,128)S(1)}) fusion(f32[1,8,32,128]{3,2,1,0:T(8,128)} %bitcast.19, f32[1,8,32,128]{3,2,1,0:T(8,128)} %bitcast.22), kind=kLoop, calls=%fused_computation.63 | loop fusion | flops 1024 | bytes 266240 | tf_op jit(solution)/shard_map/stack | solution.py:105
  1.9 3.0 %collective-permute-start = (f32[2,8,32,1]{3,2,1,0:T(8,128)S(1)}, f32[2,8,32,1]{3,2,1,0:T(8,128)S(1)}, u32[]{:S(2)}, u32[]{:S(2)}) collective-permute-start(f32[2,8,32,1]{3,2,1,0:T(8,128)S(1)} %get-tuple-element.24), channel_id=1, source_target_pairs={{0,4},{4,8},{8,12},{12,16},{16,20},{20,24},{24,28},{28,0},{1,5},{5... | collective-permute-start | bytes 6152 | tf_op jit(solution)/shard_map/ppermute | solution.py:23
  4.9 3.1 %collective-permute-start.1 = (f32[2,8,32,1]{3,2,1,0:T(8,128)S(1)}, f32[2,8,32,1]{3,2,1,0:T(8,128)S(1)}, u32[]{:S(2)}, u32[]{:S(2)}) collective-permute-start(f32[2,8,32,1]{3,2,1,0:T(8,128)S(1)} %get-tuple-element.25), channel_id=1, source_target_pairs={{4,0},{8,4},{12,8},{16,12},{20,16},{24,20},{28,24},{0,28},{5,1},{9... | collective-permute-start | bytes 6152 | tf_op jit(solution)/shard_map/ppermute | solution.py:25
  8.0 8.1 %collective-permute-done = f32[2,8,32,1]{3,2,1,0:T(8,128)S(1)} collective-permute-done((f32[2,8,32,1]{3,2,1,0:T(8,128)S(1)}, f32[2,8,32,1]{3,2,1,0:T(8,128)S(1)}, u32[]{:S(2)}, u32[]{:S(2)}) %collective-permute-start) | collective-permute-done | bytes 2080 | tf_op jit(solution)/shard_map/ppermute | solution.py:23
  16.1 2.2 %collective-permute-done.1 = f32[2,8,32,1]{3,2,1,0:T(8,128)S(1)} collective-permute-done((f32[2,8,32,1]{3,2,1,0:T(8,128)S(1)}, f32[2,8,32,1]{3,2,1,0:T(8,128)S(1)}, u32[]{:S(2)}, u32[]{:S(2)}) %collective-permute-start.1) | collective-permute-done | bytes 2080 | tf_op jit(solution)/shard_map/ppermute | solution.py:25
  18.3 0.0 copy-done
  18.3 0.0 copy-done.1
  18.3 0.2 pad_maximum_fusion.10
  18.5 2.3 %collective-permute-start.2 = (f32[2,8,2,130]{3,2,1,0:T(2,128)S(1)}, f32[2,8,2,130]{3,2,1,0:T(2,128)S(1)}, u32[]{:S(2)}, u32[]{:S(2)}) collective-permute-start(f32[2,8,2,130]{3,2,1,0:T(2,128)S(1)} %pad_maximum_fusion.9), channel_id=1, source_target_pairs={{16,0},{20,4},{24,8},{28,12},{0,16},{4,20},{8,24},{12,28},{17,1},{... | collective-permute-start | bytes 49928 | tf_op jit(solution)/shard_map/ppermute | solution.py:35
  20.9 0.0 collective-permute-start.3
  20.9 1.7 %collective-permute-start.4 = (f32[2,8,1,130]{3,2,1,0:T(1,128)S(1)}, f32[2,8,1,130]{3,2,1,0:T(1,128)S(1)}, u32[]{:S(2)}, u32[]{:S(2)}) collective-permute-start(f32[2,8,1,130]{3,2,1,0:T(1,128)S(1)} %get-tuple-element.9), channel_id=1, source_target_pairs={{1,0},{2,1},{3,2},{0,3},{5,4},{6,5},{7,6},{4,7},{9,8},{10,9},{11,1... | collective-permute-start | bytes 24968 | tf_op jit(solution)/shard_map/ppermute | solution.py:25
  22.6 1.4 %collective-permute-done.3 = f32[2,8,1,130]{3,2,1,0:T(1,128)S(1)} collective-permute-done((f32[2,8,1,130]{3,2,1,0:T(1,128)S(1)}, f32[2,8,1,130]{3,2,1,0:T(1,128)S(1)}, u32[]{:S(2)}, u32[]{:S(2)}) %collective-permute-start.3) | collective-permute-done | bytes 8352 | tf_op jit(solution)/shard_map/ppermute | solution.py:23
  24.0 0.0 collective-permute-done.4
  24.1 0.0 collective-permute-done.2
  24.1 0.3 pad_maximum_fusion
  24.4 0.0 copy-start.3
  24.4 0.0 copy-start.4
  24.5 0.8 %copy-done.3 = f32[8,32,128]{2,1,0:T(8,128)S(1)} copy-done((f32[8,32,128]{2,1,0:T(8,128)S(1)}, f32[8,32,128]{2,1,0:T(8,128)}, u32[]{:S(2)}) %copy-start.3) | copy-done | bytes 131096
  25.3 0.1 copy-done.4
  25.4 0.0 copy-start.2
  25.4 0.2 fusion.38
  25.6 0.7 %copy-done.2 = f32[8,32,128]{2,1,0:T(8,128)S(1)} copy-done((f32[8,32,128]{2,1,0:T(8,128)S(1)}, f32[8,32,128]{2,1,0:T(8,128)}, u32[]{:S(2)}) %copy-start.2) | copy-done | bytes 131096
  26.3 0.1 slice_maximum_fusion
  26.4 0.7 %collective-permute-start.5 = (f32[2,8,32,4]{3,2,1,0:T(8,128)S(1)}, f32[2,8,32,4]{3,2,1,0:T(8,128)S(1)}, u32[]{:S(2)}, u32[]{:S(2)}) collective-permute-start(f32[2,8,32,4]{3,2,1,0:T(8,128)S(1)} %get-tuple-element.22), channel_id=1, source_target_pairs={{0,4},{4,8},{8,12},{12,16},{16,20},{20,24},{24,28},{28,0},{1,5},{5... | collective-permute-start | bytes 24584 | tf_op jit(solution)/shard_map/ppermute | solution.py:23
  27.1 4.1 %collective-permute-start.6 = (f32[2,8,32,4]{3,2,1,0:T(8,128)S(1)}, f32[2,8,32,4]{3,2,1,0:T(8,128)S(1)}, u32[]{:S(2)}, u32[]{:S(2)}) collective-permute-start(f32[2,8,32,4]{3,2,1,0:T(8,128)S(1)} %get-tuple-element.23), channel_id=1, source_target_pairs={{4,0},{8,4},{12,8},{16,12},{20,16},{24,20},{28,24},{0,28},{5,1},{9... | collective-permute-start | bytes 24584 | tf_op jit(solution)/shard_map/ppermute | solution.py:25
  31.2 7.7 %collective-permute-done.5 = f32[2,8,32,4]{3,2,1,0:T(8,128)S(1)} collective-permute-done((f32[2,8,32,4]{3,2,1,0:T(8,128)S(1)}, f32[2,8,32,4]{3,2,1,0:T(8,128)S(1)}, u32[]{:S(2)}, u32[]{:S(2)}) %collective-permute-start.5) | collective-permute-done | bytes 8224 | tf_op jit(solution)/shard_map/ppermute | solution.py:23
  38.9 2.9 %collective-permute-done.6 = f32[2,8,32,4]{3,2,1,0:T(8,128)S(1)} collective-permute-done((f32[2,8,32,4]{3,2,1,0:T(8,128)S(1)}, f32[2,8,32,4]{3,2,1,0:T(8,128)S(1)}, u32[]{:S(2)}, u32[]{:S(2)}) %collective-permute-start.6) | collective-permute-done | bytes 8224 | tf_op jit(solution)/shard_map/ppermute | solution.py:25
  41.8 0.2 pad_maximum_fusion.8
  42.0 1.6 %collective-permute-start.7 = (f32[2,8,8,136]{3,2,1,0:T(8,128)S(1)}, f32[2,8,8,136]{3,2,1,0:T(8,128)S(1)}, u32[]{:S(2)}, u32[]{:S(2)}) collective-permute-start(f32[2,8,8,136]{3,2,1,0:T(8,128)S(1)} %pad_maximum_fusion.4), channel_id=1, source_target_pairs={{16,0},{20,4},{24,8},{28,12},{0,16},{4,20},{8,24},{12,28},{17,1},{... | collective-permute-start | bytes 208904 | tf_op jit(solution)/shard_map/ppermute | solution.py:35
  43.6 0.0 collective-permute-start.9
  43.6 0.5 collective-permute-start.8
  44.1 7.4 %collective-permute-done.7 = f32[2,8,8,136]{3,2,1,0:T(8,128)S(1)} collective-permute-done((f32[2,8,8,136]{3,2,1,0:T(8,128)S(1)}, f32[2,8,8,136]{3,2,1,0:T(8,128)S(1)}, u32[]{:S(2)}, u32[]{:S(2)}) %collective-permute-start.7) | collective-permute-done | bytes 69664 | tf_op jit(solution)/shard_map/ppermute | solution.py:35
  51.6 0.2 rev.6
  51.7 0.0 collective-permute-done.8
  51.7 0.2 rev.7
  51.9 0.0 collective-permute-done.9
  51.9 0.3 pad_maximum_fusion.1
  52.3 0.2 fusion.43
  52.5 0.8 %fusion.20 = f32[8,38,134]{2,1,0:T(8,128)S(1)} fusion(f32[8,40,136]{2,1,0:T(8,128)S(1)} %get-tuple-element.11, f32[8,40,136]{2,1,0:T(8,128)S(1)} %get-tuple-element.10, f32[7,38,134]{2,1,0:T(8,128)S(1)} %get-tuple-element.21, f32[7,38,134]{2,1,0:T(8,128)S(1)} %get-tuple-element.20, f32[8]{0:T(128)S(1)} %fusion.40), kind=kLoop, calls=%fused_computation.37 | loop fusion | flops 1018400 | bytes 2077568 | tf_op jit(solution)/shard_map/div | solution.py:80
  53.3 0.2 fusion.42
  53.5 0.9 %fusion.11 = f32[8,36,132]{2,1,0:T(8,128)S(1)} fusion(f32[8,38,134]{2,1,0:T(8,128)S(1)} %fusion.20, f32[8,40,136]{2,1,0:T(8,128)S(1)} %get-tuple-element.11, f32[8,40,136]{2,1,0:T(8,128)S(1)} %get-tuple-element.10, f32[7,36,132]{2,1,0:T(8,128)S(1)} %get-tuple-element.19, f32[7,36,132]{2,1,0:T(8,128)S(1)} %get-tuple-element.18, f32[8]{0:T(128)S(1)} %fusion.40), kind=kLoop, calls=%fused_computation.21 | loop fusion | flops 950400 | bytes 1938848 | tf_op jit(solution)/shard_map/div | solution.py:80
  54.4 0.2 fusion.41
  54.6 0.9 %fusion.2 = f32[8,34,130]{2,1,0:T(8,128)S(1)} fusion(f32[8,36,132]{2,1,0:T(8,128)S(1)} %fusion.11, f32[8,40,136]{2,1,0:T(8,128)S(1)} %get-tuple-element.11, f32[8,40,136]{2,1,0:T(8,128)S(1)} %get-tuple-element.10, f32[7,34,130]{2,1,0:T(8,128)S(1)} %get-tuple-element.17, f32[7,34,130]{2,1,0:T(8,128)S(1)} %get-tuple-element.16, f32[8]{0:T(128)S(1)} %fusion.40), kind=kLoop, calls=%fused_computation.5 | loop fusion | flops 884000 | bytes 1803392 | tf_op jit(solution)/shard_map/div | solution.py:80
  55.5 1.0 %multiply_subtract_fusion = (f32[8,32,128]{2,1,0:T(8,128)}, f32[8,32,128]{2,1,0:T(8,128)}, f32[8,32,128]{2,1,0:T(8,128)}, f32[8,32,128]{2,1,0:T(8,128)}) fusion(f32[8,32,128]{2,1,0:T(8,128)S(1)} %copy-done.3, f32[8,32,128]{2,1,0:T(8,128)S(1)} %copy-done.4, f32[8,34,130]{2,1,0:T(8,128)S(1)} %fusion.2, f32[8,32,128]{2,1,0:T(8,128)S(1)} %copy-done.1, ...), kind=kLoop, calls=%fused_computation.78 | loop fusion | flops 294912 | bytes 1703936 | tf_op jit(solution)/shard_map/sub | solution.py:114
  (9 shorter events, 0.3 us)
Async XLA Ops:
  0.6 17.7 %copy-start = (f32[8,32,128]{2,1,0:T(8,128)S(1)}, f32[8,32,128]{2,1,0:T(8,128)}, u32[]{:S(2)}) copy-start(f32[8,32,128]{2,1,0:T(8,128)} %param.8) | copy-start | bytes 393220
  0.6 17.7 %copy-start.1 = (f32[8,32,128]{2,1,0:T(8,128)S(1)}, f32[8,32,128]{2,1,0:T(8,128)}, u32[]{:S(2)}) copy-start(f32[8,32,128]{2,1,0:T(8,128)} %param.7) | copy-start | bytes 393220
  1.9 14.2 %collective-permute-start = (f32[2,8,32,1]{3,2,1,0:T(8,128)S(1)}, f32[2,8,32,1]{3,2,1,0:T(8,128)S(1)}, u32[]{:S(2)}, u32[]{:S(2)}) collective-permute-start(f32[2,8,32,1]{3,2,1,0:T(8,128)S(1)} %get-tuple-element.24), channel_id=1, source_target_pairs={{0,4},{4,8},{8,12},{12,16},{16,20},{20,24},{24,28},{28,0},{1,5},{5... | collective-permute-start | bytes 6152 | tf_op jit(solution)/shard_map/ppermute | solution.py:23
  4.9 13.4 %collective-permute-start.1 = (f32[2,8,32,1]{3,2,1,0:T(8,128)S(1)}, f32[2,8,32,1]{3,2,1,0:T(8,128)S(1)}, u32[]{:S(2)}, u32[]{:S(2)}) collective-permute-start(f32[2,8,32,1]{3,2,1,0:T(8,128)S(1)} %get-tuple-element.25), channel_id=1, source_target_pairs={{4,0},{8,4},{12,8},{16,12},{20,16},{24,20},{28,24},{0,28},{5,1},{9... | collective-permute-start | bytes 6152 | tf_op jit(solution)/shard_map/ppermute | solution.py:25
  18.5 5.5 %collective-permute-start.2 = (f32[2,8,2,130]{3,2,1,0:T(2,128)S(1)}, f32[2,8,2,130]{3,2,1,0:T(2,128)S(1)}, u32[]{:S(2)}, u32[]{:S(2)}) collective-permute-start(f32[2,8,2,130]{3,2,1,0:T(2,128)S(1)} %pad_maximum_fusion.9), channel_id=1, source_target_pairs={{16,0},{20,4},{24,8},{28,12},{0,16},{4,20},{8,24},{12,28},{17,1},{... | collective-permute-start | bytes 49928 | tf_op jit(solution)/shard_map/ppermute | solution.py:35
  20.9 3.2 %collective-permute-start.3 = (f32[2,8,1,130]{3,2,1,0:T(1,128)S(1)}, f32[2,8,1,130]{3,2,1,0:T(1,128)S(1)}, u32[]{:S(2)}, u32[]{:S(2)}) collective-permute-start(f32[2,8,1,130]{3,2,1,0:T(1,128)S(1)} %get-tuple-element.8), channel_id=1, source_target_pairs={{0,1},{1,2},{2,3},{3,0},{4,5},{5,6},{6,7},{7,4},{8,9},{9,10},{10,1... | collective-permute-start | bytes 24968 | tf_op jit(solution)/shard_map/ppermute | solution.py:23
  20.9 3.2 %collective-permute-start.4 = (f32[2,8,1,130]{3,2,1,0:T(1,128)S(1)}, f32[2,8,1,130]{3,2,1,0:T(1,128)S(1)}, u32[]{:S(2)}, u32[]{:S(2)}) collective-permute-start(f32[2,8,1,130]{3,2,1,0:T(1,128)S(1)} %get-tuple-element.9), channel_id=1, source_target_pairs={{1,0},{2,1},{3,2},{0,3},{5,4},{6,5},{7,6},{4,7},{9,8},{10,9},{11,1... | collective-permute-start | bytes 24968 | tf_op jit(solution)/shard_map/ppermute | solution.py:25
  24.4 0.9 %copy-start.3 = (f32[8,32,128]{2,1,0:T(8,128)S(1)}, f32[8,32,128]{2,1,0:T(8,128)}, u32[]{:S(2)}) copy-start(f32[8,32,128]{2,1,0:T(8,128)} %param.9) | copy-start | bytes 393220
  24.4 1.0 %copy-start.4 = (f32[8,32,128]{2,1,0:T(8,128)S(1)}, f32[8,32,128]{2,1,0:T(8,128)}, u32[]{:S(2)}) copy-start(f32[8,32,128]{2,1,0:T(8,128)} %param.10) | copy-start | bytes 393220
  25.4 0.9 %copy-start.2 = (f32[8,32,128]{2,1,0:T(8,128)S(1)}, f32[8,32,128]{2,1,0:T(8,128)}, u32[]{:S(2)}) copy-start(f32[8,32,128]{2,1,0:T(8,128)} %param.11) | copy-start | bytes 393220
  26.4 12.4 %collective-permute-start.5 = (f32[2,8,32,4]{3,2,1,0:T(8,128)S(1)}, f32[2,8,32,4]{3,2,1,0:T(8,128)S(1)}, u32[]{:S(2)}, u32[]{:S(2)}) collective-permute-start(f32[2,8,32,4]{3,2,1,0:T(8,128)S(1)} %get-tuple-element.22), channel_id=1, source_target_pairs={{0,4},{4,8},{8,12},{12,16},{16,20},{20,24},{24,28},{28,0},{1,5},{5... | collective-permute-start | bytes 24584 | tf_op jit(solution)/shard_map/ppermute | solution.py:23
  27.1 14.6 %collective-permute-start.6 = (f32[2,8,32,4]{3,2,1,0:T(8,128)S(1)}, f32[2,8,32,4]{3,2,1,0:T(8,128)S(1)}, u32[]{:S(2)}, u32[]{:S(2)}) collective-permute-start(f32[2,8,32,4]{3,2,1,0:T(8,128)S(1)} %get-tuple-element.23), channel_id=1, source_target_pairs={{4,0},{8,4},{12,8},{16,12},{20,16},{24,20},{28,24},{0,28},{5,1},{9... | collective-permute-start | bytes 24584 | tf_op jit(solution)/shard_map/ppermute | solution.py:25
  42.0 9.6 %collective-permute-start.7 = (f32[2,8,8,136]{3,2,1,0:T(8,128)S(1)}, f32[2,8,8,136]{3,2,1,0:T(8,128)S(1)}, u32[]{:S(2)}, u32[]{:S(2)}) collective-permute-start(f32[2,8,8,136]{3,2,1,0:T(8,128)S(1)} %pad_maximum_fusion.4), channel_id=1, source_target_pairs={{16,0},{20,4},{24,8},{28,12},{0,16},{4,20},{8,24},{12,28},{17,1},{... | collective-permute-start | bytes 208904 | tf_op jit(solution)/shard_map/ppermute | solution.py:35
  43.6 8.3 %collective-permute-start.9 = (f32[2,8,4,136]{3,2,1,0:T(4,128)S(1)}, f32[2,8,4,136]{3,2,1,0:T(4,128)S(1)}, u32[]{:S(2)}, u32[]{:S(2)}) collective-permute-start(f32[2,8,4,136]{3,2,1,0:T(4,128)S(1)} %get-tuple-element.6), channel_id=1, source_target_pairs={{1,0},{2,1},{3,2},{0,3},{5,4},{6,5},{7,6},{4,7},{9,8},{10,9},{11,1... | collective-permute-start | bytes 104456 | tf_op jit(solution)/shard_map/ppermute | solution.py:25
  43.6 8.1 %collective-permute-start.8 = (f32[2,8,4,136]{3,2,1,0:T(4,128)S(1)}, f32[2,8,4,136]{3,2,1,0:T(4,128)S(1)}, u32[]{:S(2)}, u32[]{:S(2)}) collective-permute-start(f32[2,8,4,136]{3,2,1,0:T(4,128)S(1)} %get-tuple-element.7), channel_id=1, source_target_pairs={{0,1},{1,2},{2,3},{3,0},{4,5},{5,6},{6,7},{7,4},{8,9},{9,10},{10,1... | collective-permute-start | bytes 104456 | tf_op jit(solution)/shard_map/ppermute | solution.py:23
where the time goes:
time: 56.6 us; the launch traced here: 56.5 us
  waiting for transfers between devices  29.7 us (52%)
  starting transfers between devices  17.1 us (30%)
  other arithmetic  6.15 us (11%)
  local copies, waits for them, and re-layouts  2.7 us (5%)
  between operations  0.83 us (1%)
    ppermute x4, waiting for transfers between devices, with_halo(): lax.ppermute(tail, axis, [(i, (i + 1) % count) for i in range(count)])  17.2 us
    ppermute x4, starting transfers between devices, with_halo(): lax.ppermute(head, axis, [((i + 1) % count, i) for i in range(count)])  8.95 us
    ppermute x2, waiting for transfers between devices, passed_along(): return lax.ppermute(block, axis, route)  7.41 us
    ppermute x4, waiting for transfers between devices, with_halo(): lax.ppermute(head, axis, [((i + 1) % count, i) for i in range(count)])  5.1 us
    ppermute x4, starting transfers between devices, with_halo(): lax.ppermute(tail, axis, [(i, (i + 1) % count) for i in range(count)])  4.21 us
    ppermute x2, starting transfers between devices, passed_along(): return lax.ppermute(block, axis, route)  3.94 us
    div x3, other arithmetic, jacobi(): return numerator / denominator  2.48 us
    unnamed x10, local copies, waits for them, and re-layouts  1.64 us
  transfers between devices with their start and end apart: 10, of which 6 were waited for; matrix products, arithmetic and copies ran while one was open for 1% of the time, Pallas kernels for 0%

commit v1 on v0

v1 whole, which is shorter than its diff:
```python
import functools

import jax
import jax.numpy as jnp
from jax import lax
from jax.experimental import pallas as pl
from jax.experimental.pallas import tpu as pltpu
from jax.sharding import PartitionSpec as P

SWEEPS = 3
HALO = SWEEPS + 1
LANES = 128
EDGE = 8 * HALO
MESH = pl.DeviceIdType.MESH

divergence_weight = 0.5
thermal_weight = 0.3
vertical_coupling = 0.5
gradient_weight = 0.5
adjust_weight = 0.5


def lane_of(rows):
    return lax.broadcasted_iota(jnp.int32, (rows, LANES), 1)


def turn(x, shift, axis=1):
    shift = shift % x.shape[axis]
    return x if shift == 0 else pltpu.roll(x, shift, axis)


def halo_kernel(
    nlon, nlat, u_ref, v_ref, t_ref, p_ref, k_ref,
    ns_ref, ew_ref, cn_ref, own_ref, ns_send, send_sem, recv_sem,
):
    levels, rows, _ = u_ref.shape
    lon, lat = lax.axis_index("lon"), lax.axis_index("lat")
    poles = (lat == 0, lat == nlat - 1)

    def partner(side, shift):
        pole = poles[side]
        row = jnp.where(pole, lat, lat + (1 if side else -1))
        col = lax.rem(lon + shift + nlon + jnp.where(pole, nlon // 2, 0), nlon)
        return {"lon": col, "lat": row}

    def beside(shift):
        return {"lon": lax.rem(lon + shift + nlon, nlon), "lat": lat}

    everyone = [beside(-1), beside(1)]
    everyone += [partner(side, shift) for side in (0, 1) for shift in (-1, 0, 1)]
    barrier = pltpu.get_barrier_semaphore()
    for device in everyone:
        pl.semaphore_signal(barrier, inc=1, device_id=device, device_id_type=MESH)

    lane = lane_of(rows)
    group = lane // HALO
    row_id = lax.broadcasted_iota(jnp.int32, (rows, LANES), 0)
    place = [[jnp.where(poles[s], HALO - 1 - r, r) for r in range(HALO)] for s in (0, 1)]
    first = (0, rows - HALO)
    signs = [jnp.where(poles[s], -1.0, 1.0).astype(jnp.float32) for s in (0, 1)]
    west = jnp.zeros((rows, LANES), jnp.float32)
    east = jnp.zeros((rows, LANES), jnp.float32)
    for level in range(levels):
        u, v, k = u_ref[level], v_ref[level], k_ref[level]
        u_diff = jnp.where(lane == LANES - 1, 0.0, turn(u, -1)) - jnp.where(lane == 0, 0.0, turn(u, 1))
        v_diff = jnp.where(row_id == rows - 1, 0.0, turn(v, -1, 0)) - jnp.where(row_id == 0, 0.0, turn(v, 1, 0))
        part = p_ref[level] - 0.5 * divergence_weight * (u_diff + v_diff) + thermal_weight * t_ref[level]
        for index, field in enumerate((part, k, u, v)):
            slot = index * levels + level
            moved = turn(field, (slot + 1) * HALO)
            east = jnp.where(group == slot, moved, east)
            west = jnp.where(group == (slot + 1) % (LANES // HALO), moved, west)
        for s in (0, 1):
            for r in range(HALO):
                here = slice(first[s] + r, first[s] + r + 1)
                ns_send[s, pl.ds(level * HALO + place[s][r], 1)] = part[here]
                ns_send[s, pl.ds(EDGE + level * HALO + place[s][r], 1)] = k[here]
            edge = slice(0, 1) if s == 0 else slice(rows - 1, rows)
            ns_send[s, 2 * EDGE + level : 2 * EDGE + level + 1] = v[edge] * signs[s]
    west = turn(west, -HALO)
    own_ref[0] = west
    own_ref[1] = east
    base = 2 * EDGE + levels
    for s in (0, 1):
        flip = jnp.where(lane_of(1) >= 3 * EDGE, signs[s], 1.0)
        for r in range(HALO):
            here = slice(first[s] + r, first[s] + r + 1)
            ns_send[s, pl.ds(base + place[s][r], 1)] = west[here] * flip
            ns_send[s, pl.ds(base + HALO + place[s][r], 1)] = east[here] * flip

    pl.semaphore_wait(barrier, len(everyone))
    copies = []

    def send(src, dst, device, out, into):
        copy = pltpu.make_async_remote_copy(
            src_ref=src, dst_ref=dst, send_sem=send_sem.at[out], recv_sem=recv_sem.at[into],
            device_id=device, device_id_type=MESH,
        )
        copy.start()
        copies.append(copy)

    def arrive(dst, into):
        pltpu.make_async_remote_copy(
            src_ref=dst, dst_ref=dst, send_sem=send_sem.at[0], recv_sem=recv_sem.at[into],
            device_id=beside(1), device_id_type=MESH,
        ).wait_recv()

    for s in (0, 1):
        there = jnp.where(poles[s], s, 1 - s)
        send(ns_send.at[s], ns_ref.at[there], partner(s, 0), 2 + s, 2 + there)
        corner = ns_send.at[s, pl.ds(base, 2 * HALO)]
        send(corner, cn_ref.at[there, 1], partner(s, -1), 4 + 2 * s, 4 + 2 * there + 1)
        send(corner, cn_ref.at[there, 0], partner(s, 1), 5 + 2 * s, 4 + 2 * there)
    send(own_ref.at[0], ew_ref.at[1], beside(-1), 0, 1)
    send(own_ref.at[1], ew_ref.at[0], beside(1), 1, 0)
    for side in (0, 1):
        arrive(ew_ref.at[side], side)
        arrive(ns_ref.at[side], 2 + side)
        arrive(cn_ref.at[side, 0], 4 + 2 * side)
        arrive(cn_ref.at[side, 1], 5 + 2 * side)
    for copy in copies:
        copy.wait_send()


def step_kernel(
    u_ref, v_ref, t_ref, p_ref, k_ref, ns_ref, ew_ref, cn_ref, own_ref,
    zonal_ref, meridional_ref, theta_ref, next_ref,
    tall, v_tall, k_tall, source, coef, xa, xb,
):
    levels, rows, _ = u_ref.shape
    high = rows + 2 * HALO
    pad = 8
    core = slice(HALO, HALO + rows)
    base = 2 * EDGE + levels
    top = HALO + rows

    tall[0, core], tall[1, core] = ew_ref[0], own_ref[0]
    tall[2, core], tall[3, core] = own_ref[1], ew_ref[1]
    for s in (0, 1):
        rim = slice(0, HALO) if s == 0 else slice(top, high)
        tall[0, rim] = cn_ref[s, 0, HALO : 2 * HALO]
        tall[1, rim] = ns_ref[s, base : base + HALO]
        tall[2, rim] = ns_ref[s, base + HALO : base + 2 * HALO]
        tall[3, rim] = cn_ref[s, 1, :HALO]

    lane = lane_of(high)
    part, column = lane // EDGE, lane % HALO
    level_id = (lane % EDGE) // HALO
    row_id = lax.broadcasted_iota(jnp.int32, (high, LANES), 0)
    parts = [tall[i] for i in range(4)]

    def side_field(index):
        moved = [turn(parts[i], (i - index) * EDGE) for i in range(4)]
        return jnp.where(part < 2, jnp.where(part == 0, moved[0], moved[1]), jnp.where(part == 2, moved[2], moved[3]))

    def side_east(x):
        return jnp.where(column == HALO - 1, turn(x, HALO - 1 - EDGE), turn(x, -1))

    def side_west(x):
        return jnp.where(column == 0, turn(x, EDGE - HALO + 1), turn(x, 1))

    def fix_rows(partial, v):
        lack_north = (row_id == HALO - 1) | (row_id == top - 1)
        lack_south = (row_id == HALO) | (row_id == top)
        return partial - jnp.where(lack_north, 0.25 * turn(v, -1, 0), 0.0) + jnp.where(lack_south, 0.25 * turn(v, 1, 0), 0.0)

    side_p, side_k, side_u, side_v = [side_field(i) for i in range(4)]
    lack_east = (column == HALO - 1) & (part % 2 == 0)
    lack_west = (column == 0) & (part % 2 == 1)
    side_s = side_p - jnp.where(lack_east, 0.25 * side_east(side_u), 0.0) + jnp.where(lack_west, 0.25 * side_west(side_u), 0.0)
    side_s = fix_rows(side_s, side_v)
    se = 0.5 * (side_k + side_east(side_k))
    sw = 0.5 * (side_k + side_west(side_k))
    sn = 0.5 * (side_k + turn(side_k, -1, 0))
    ss = 0.5 * (side_k + turn(side_k, 1, 0))
    rim_level = (level_id == 0) | (level_id == levels - 1)
    inverse = 1.0 / (1.0 + se + sw + sn + ss + jnp.where(rim_level, vertical_coupling, 2.0 * vertical_coupling))
    se, sw, sn, ss = se * inverse, sw * inverse, sn * inverse, ss * inverse
    s0 = side_s * inverse
    up = jnp.where(level_id == levels - 1, 0.0, vertical_coupling * inverse)
    down = jnp.where(level_id == 0, 0.0, vertical_coupling * inverse)
    side = [side_s]
    for _ in range(SWEEPS):
        x = side[-1]
        side.append(
            s0 + se * side_east(x) + sw * side_west(x) + sn * turn(x, -1, 0) + ss * turn(x, 1, 0)
            + up * turn(x, -HALO) + down * turn(x, HALO)
        )

    def from_west(x, level):
        return turn(x, -(level * HALO + HALO - 1))

    def from_east(x, level):
        return turn(x, LANES - 1 - 3 * EDGE - level * HALO)

    def east_of(x, beyond, level):
        return jnp.where(lane == LANES - 1, from_east(beyond, level), turn(x, -1))

    def west_of(x, beyond, level):
        return jnp.where(lane == 0, from_west(beyond, level), turn(x, 1))

    here = slice(pad, pad + high)
    north, south = slice(pad + 1, pad + 1 + high), slice(pad - 1, pad - 1 + high)
    zero_row = jnp.zeros((1, LANES), jnp.float32)
    lane_core = lane_of(rows)
    for level in range(levels):
        for ref in (xa, xb):
            ref[level, pad - 1 : pad] = zero_row
            ref[level, pad + high : pad + high + 1] = zero_row
        for s, start in ((0, 0), (1, top)):
            source[level, start : start + HALO] = ns_ref[s, level * HALO : (level + 1) * HALO]
            k_tall[level, pad + start : pad + start + HALO] = ns_ref[s, EDGE + level * HALO : EDGE + (level + 1) * HALO]
        k_tall[level, pad - 1 : pad] = zero_row
        k_tall[level, pad + high : pad + high + 1] = zero_row
        k_tall[level, pad + HALO : pad + top] = k_ref[level]
        u, v = u_ref[level], v_ref[level]
        v_tall[HALO - 1 : HALO] = ns_ref[0, 2 * EDGE + level : 2 * EDGE + level + 1]
        v_tall[top : top + 1] = ns_ref[1, 2 * EDGE + level : 2 * EDGE + level + 1]
        v_tall[core] = v
        v_diff = v_tall[HALO + 1 : top + 1] - v_tall[HALO - 1 : top - 1]
        u_diff = jnp.where(lane_core == LANES - 1, 0.0, turn(u, -1)) - jnp.where(lane_core == 0, 0.0, turn(u, 1))
        source[level, core] = p_ref[level] - 0.5 * divergence_weight * (u_diff + v_diff) + thermal_weight * t_ref[level]
        source[level, HALO - 1 : HALO] = source[level, HALO - 1 : HALO] - 0.25 * v[:1]
        source[level, top : top + 1] = source[level, top : top + 1] + 0.25 * v[rows - 1 :]
        full = (
            source[level]
            + jnp.where(lane == 0, 0.25 * from_west(side_u, level), 0.0)
            - jnp.where(lane == LANES - 1, 0.25 * from_east(side_u, level), 0.0)
        )
        k = k_tall[level, here]
        ke = 0.5 * (k + east_of(k, side_k, level))
        kw = 0.5 * (k + west_of(k, side_k, level))
        kn = 0.5 * (k + k_tall[level, north])
        ks = 0.5 * (k + k_tall[level, south])
        count = vertical_coupling * ((level > 0) + (level < levels - 1))
        inv = 1.0 / (1.0 + ke + kw + kn + ks + count)
        xa[level, here] = full
        for index, value in enumerate((full * inv, ke * inv, kw * inv, kn * inv, ks * inv, vertical_coupling * inv)):
            coef[index, level] = value

    now, later = xa, xb
    for sweep in range(SWEEPS):
        beyond = side[sweep]
        for level in range(levels):
            x = now[level, here]
            if level == 0:
                column_sum = now[1, here]
            elif level == levels - 1:
                column_sum = now[level - 1, here]
            else:
                column_sum = now[level + 1, here] + now[level - 1, here]
            later[level, here] = (
                coef[0, level]
                + coef[1, level] * east_of(x, beyond, level)
                + coef[2, level] * west_of(x, beyond, level)
                + coef[3, level] * now[level, north]
                + coef[4, level] * now[level, south]
                + coef[5, level] * column_sum
            )
        now, later = later, now

    lane = lane_core
    beyond = side[SWEEPS][core]
    own = pad + HALO
    for level in range(levels):
        x = now[level, own : own + rows]
        next_ref[level] = x
        zonal_ref[level] = u_ref[level] - 0.5 * gradient_weight * (east_of(x, beyond, level) - west_of(x, beyond, level))
        north_south = now[level, own + 1 : own + 1 + rows] - now[level, own - 1 : own - 1 + rows]
        meridional_ref[level] = v_ref[level] - 0.5 * gradient_weight * north_south
        theta_ref[level] = t_ref[level] - adjust_weight * (x - p_ref[level])


def on_device(nlon, nlat, *fields):
    levels, rows, columns = fields[0].shape
    assert (levels, columns) == (8, LANES)
    f32 = jnp.float32
    vmem = pl.BlockSpec(memory_space=pltpu.VMEM)
    length = 2 * EDGE + levels + 2 * HALO
    high = rows + 2 * HALO
    shapes = [(2, length, LANES), (2, rows, LANES), (2, 2, 2 * HALO, LANES), (2, rows, LANES)]
    halos = pl.pallas_call(
        functools.partial(halo_kernel, nlon, nlat),
        out_shape=[jax.ShapeDtypeStruct(s, f32) for s in shapes],
        in_specs=[vmem] * 5,
        out_specs=[vmem] * 4,
        scratch_shapes=[
            pltpu.VMEM((2, length, LANES), f32),
            pltpu.SemaphoreType.DMA((8,)),
            pltpu.SemaphoreType.DMA((8,)),
        ],
        compiler_params=pltpu.CompilerParams(collective_id=0, has_side_effects=True),
        name="halo",
    )(*fields)
    outputs = pl.pallas_call(
        step_kernel,
        out_shape=[jax.ShapeDtypeStruct((levels, rows, LANES), f32)] * 4,
        in_specs=[vmem] * 9,
        out_specs=[vmem] * 4,
        scratch_shapes=[
            pltpu.VMEM((4, high, LANES), f32),
            pltpu.VMEM((high, LANES), f32),
            pltpu.VMEM((levels, high + 16, LANES), f32),
            pltpu.VMEM((levels, high, LANES), f32),
            pltpu.VMEM((6, levels, high, LANES), f32),
            pltpu.VMEM((levels, high + 16, LANES), f32),
            pltpu.VMEM((levels, high + 16, LANES), f32),
        ],
        name="step",
    )(*fields, *halos)
    return tuple(outputs)


def solution(mesh):
    spec = P(None, "lat", "lon")
    return jax.shard_map(
        functools.partial(on_device, mesh.shape["lon"], mesh.shape["lat"]),
        mesh=mesh,
        in_specs=(spec,) * 5,
        out_specs=(spec,) * 4,
        check_vma=False,
    )
```

time: 56.6 us -> 15.6 us (0.28)
  waiting for transfers between devices: 29.7 us -> 0 us
  starting transfers between devices: 17.1 us -> 0 us
  Pallas kernels: 0 us -> 14.8 us
  other arithmetic: 6.15 us -> 0 us
  local copies, waits for them, and re-layouts: 2.7 us -> 0 us
    ppermute x10 -> x0, waiting for transfers between devices: 29.7 us -> none  [the longest x4 17.2 us: with_halo(): lax.ppermute(tail, axis, [(i, (i + 1) % count) for i in range(count)])]
    ppermute x10 -> x0, starting transfers between devices: 17.1 us -> none  [the longest x4 8.95 us: with_halo(): lax.ppermute(head, axis, [((i + 1) % count, i) for i in range(count)])]
    pallas_call x0 -> x2, Pallas kernels: none -> 14.8 us  [the longest x1 11.5 us: on_device(): pl.pallas_call(functools.partial(halo_kernel, nlon, nlat), out_shape=[jax...]
    div x3 -> x0, other arithmetic: 2.48 us -> none  [jacobi(): return numerator / denominator]
    unnamed x10 -> x0, local copies, waits for them, and re-layouts: 1.64 us -> none
    another operation x3 -> x0, other arithmetic: 1.57 us -> none  [the longest x1 1.26 us: on_device(): winds = extend(jnp.stack([zonal_wind, meridional_wind]), [-1.0, -1.0], 1)]
    sub x1 -> x0, other arithmetic: 0.97 us -> none  [on_device(): theta_next = theta_field - adjust_weight * (iterate - pressure)]
    concatenate x5 -> x0, other arithmetic: 0.89 us -> none  [the longest x2 0.65 us: extend(): jnp.concatenate([lower_rim, padded[:, :, margin:-margin], upper_rim], axi...]
  transfers between devices with their start and end apart: 10 -> 0, of which waited for: 6 -> 0; matrix products, arithmetic and copies ran while one was open for 1% -> 0% of each run, Pallas kernels for 0% -> 0%
where the time goes in v1:
time: 15.6 us; the launch traced here: 15.5 us
  Pallas kernels  14.8 us (95%)
  between operations  0.64 us (4%)
    pallas_call x1, Pallas kernels, on_device(): pl.pallas_call(functools.partial(halo_kernel, nlon, nlat), out_shape=[jax...  11.5 us
    pallas_call x1, Pallas kernels, on_device(): pl.pallas_call(step_kernel, out_shape=[jax.ShapeDtypeStruct((levels, rows...  3.34 us

profile of v1, /device:TPU:0, one launch (start us, length us, event | category | flops | bytes accessed | tf_op | source)
XLA Modules:
  0.0 15.5 jit_solution(16032544744757578855)
XLA Ops:
  0.6 11.5 %halo.1 = (f32[2,80,128]{2,1,0:T(8,128)}, f32[2,32,128]{2,1,0:T(8,128)}, f32[2,2,8,128]{3,2,1,0:T(8,128)}, f32[2,32,128]{2,1,0:T(8,128)}) custom-call(f32[8,32,128]{2,1,0:T(8,128)} %u_ref.3, f32[8,32,128]{2,1,0:T(8,128)} %v_ref.3, f32[8,32,128]{2,1,0:T(8,128)} %t_ref.3, f32[8,32,128]{2,1,0:T(8,128)} %p_ref.3, f32[8,32,128]{2,1,0:T(8,128)} %k_ref.3), custom_call_target="tpu_custom_call" | custom-call | tf_op jit(solution)/shard_map/halo/pallas_call | solution.py:282
  12.1 3.3 %step.1 = (f32[8,32,128]{2,1,0:T(8,128)}, f32[8,32,128]{2,1,0:T(8,128)}, f32[8,32,128]{2,1,0:T(8,128)}, f32[8,32,128]{2,1,0:T(8,128)}) custom-call(f32[8,32,128]{2,1,0:T(8,128)} %u_ref.3, f32[8,32,128]{2,1,0:T(8,128)} %v_ref.3, f32[8,32,128]{2,1,0:T(8,128)} %t_ref.3, f32[8,32,128]{2,1,0:T(8,128)} %p_ref.3, f32[8,32,128]{2,1,0:T(8,128)} %k_ref.3, ...), custom_call_target="tpu_custom_call" | custom-call | tf_op jit(solution)/shard_map/step/pallas_call | solution.py:295

commit v2 on v1

--- a/solution.py
+++ b/solution.py
@@ -9,7 +9,9 @@
 
 SWEEPS = 3
 HALO = SWEEPS + 1
+CHUNK = 2
 LANES = 128
+PAD = 8
 EDGE = 8 * HALO
 MESH = pl.DeviceIdType.MESH
 
@@ -29,11 +31,13 @@
     return x if shift == 0 else pltpu.roll(x, shift, axis)
 
 
-def halo_kernel(
-    nlon, nlat, u_ref, v_ref, t_ref, p_ref, k_ref,
-    ns_ref, ew_ref, cn_ref, own_ref, ns_send, send_sem, recv_sem,
+def kernel(
+    nlon, nlat, u_hbm, v_hbm, t_hbm, p_hbm, k_hbm,
+    xb, side_ref, u_ref, v_tall, t_ref, p_ref,
+    k_tall, ns_ref, ew_ref, cn_ref, own_ref, ns_send,
+    tall, source, coef, xa, load_sem, send_sem, recv_sem,
 ):
-    levels, rows, _ = u_ref.shape
+    levels, rows, _ = t_ref.shape
     lon, lat = lax.axis_index("lon"), lax.axis_index("lat")
     poles = (lat == 0, lat == nlat - 1)
 
@@ -52,6 +56,18 @@
     for device in everyone:
         pl.semaphore_signal(barrier, inc=1, device_id=device, device_id_type=MESH)
 
+    loads = [
+        pltpu.make_async_copy(src, dst, load_sem.at[i])
+        for i, (src, dst) in enumerate((
+            (u_hbm, u_ref), (v_hbm, v_tall.at[:, pl.ds(PAD, rows)]), (t_hbm, t_ref),
+            (p_hbm, p_ref), (k_hbm, k_tall.at[:, pl.ds(PAD, rows)]),
+        ))
+    ]
+    for load in loads:
+        load.start()
+    for load in loads:
+        load.wait()
+    inner = slice(PAD, PAD + rows)
     lane = lane_of(rows)
     group = lane // HALO
     row_id = lax.broadcasted_iota(jnp.int32, (rows, LANES), 0)
@@ -61,10 +77,11 @@
     west = jnp.zeros((rows, LANES), jnp.float32)
     east = jnp.zeros((rows, LANES), jnp.float32)
     for level in range(levels):
-        u, v, k = u_ref[level], v_ref[level], k_ref[level]
+        u, v, k = u_ref[level], v_tall[level, inner], k_tall[level, inner]
         u_diff = jnp.where(lane == LANES - 1, 0.0, turn(u, -1)) - jnp.where(lane == 0, 0.0, turn(u, 1))
         v_diff = jnp.where(row_id == rows - 1, 0.0, turn(v, -1, 0)) - jnp.where(row_id == 0, 0.0, turn(v, 1, 0))
         part = p_ref[level] - 0.5 * divergence_weight * (u_diff + v_diff) + thermal_weight * t_ref[level]
+        source[level, inner] = part
         for index, field in enumerate((part, k, u, v)):
             slot = index * levels + level
             moved = turn(field, (slot + 1) * HALO)
@@ -118,21 +135,11 @@
         arrive(ns_ref.at[side], 2 + side)
         arrive(cn_ref.at[side, 0], 4 + 2 * side)
         arrive(cn_ref.at[side, 1], 5 + 2 * side)
-    for copy in copies:
-        copy.wait_send()
-
-
-def step_kernel(
-    u_ref, v_ref, t_ref, p_ref, k_ref, ns_ref, ew_ref, cn_ref, own_ref,
-    zonal_ref, meridional_ref, theta_ref, next_ref,
-    tall, v_tall, k_tall, source, coef, xa, xb,
-):
-    levels, rows, _ = u_ref.shape
+
     high = rows + 2 * HALO
-    pad = 8
     core = slice(HALO, HALO + rows)
-    base = 2 * EDGE + levels
     top = HALO + rows
+    bottom = PAD - HALO
 
     tall[0, core], tall[1, core] = ew_ref[0], own_ref[0]
     tall[2, core], tall[3, core] = own_ref[1], ew_ref[1]
@@ -199,31 +206,23 @@
     def west_of(x, beyond, level):
         return jnp.where(lane == 0, from_west(beyond, level), turn(x, 1))
 
-    here = slice(pad, pad + high)
-    north, south = slice(pad + 1, pad + 1 + high), slice(pad - 1, pad - 1 + high)
+    here = slice(bottom, bottom + high)
+    north, south = slice(bottom + 1, bottom + 1 + high), slice(bottom - 1, bottom - 1 + high)
     zero_row = jnp.zeros((1, LANES), jnp.float32)
-    lane_core = lane_of(rows)
     for level in range(levels):
-        for ref in (xa, xb):
-            ref[level, pad - 1 : pad] = zero_row
-            ref[level, pad + high : pad + high + 1] = zero_row
-        for s, start in ((0, 0), (1, top)):
+        for ref in (xa, xb, k_tall):
+            ref[level, bottom - 1 : bottom] = zero_row
+            ref[level, bottom + high : bottom + high + 1] = zero_row
+        for s, start in ((0, bottom), (1, PAD + rows)):
             source[level, start : start + HALO] = ns_ref[s, level * HALO : (level + 1) * HALO]
-            k_tall[level, pad + start : pad + start + HALO] = ns_ref[s, EDGE + level * HALO : EDGE + (level + 1) * HALO]
-        k_tall[level, pad - 1 : pad] = zero_row
-        k_tall[level, pad + high : pad + high + 1] = zero_row
-        k_tall[level, pad + HALO : pad + top] = k_ref[level]
-        u, v = u_ref[level], v_ref[level]
-        v_tall[HALO - 1 : HALO] = ns_ref[0, 2 * EDGE + level : 2 * EDGE + level + 1]
-        v_tall[top : top + 1] = ns_ref[1, 2 * EDGE + level : 2 * EDGE + level + 1]
-        v_tall[core] = v
-        v_diff = v_tall[HALO + 1 : top + 1] - v_tall[HALO - 1 : top - 1]
-        u_diff = jnp.where(lane_core == LANES - 1, 0.0, turn(u, -1)) - jnp.where(lane_core == 0, 0.0, turn(u, 1))
-        source[level, core] = p_ref[level] - 0.5 * divergence_weight * (u_diff + v_diff) + thermal_weight * t_ref[level]
-        source[level, HALO - 1 : HALO] = source[level, HALO - 1 : HALO] - 0.25 * v[:1]
-        source[level, top : top + 1] = source[level, top : top + 1] + 0.25 * v[rows - 1 :]
+            k_tall[level, start : start + HALO] = ns_ref[s, EDGE + level * HALO : EDGE + (level + 1) * HALO]
+        for s, (outer, inside) in enumerate(((PAD - 1, PAD), (PAD + rows, PAD + rows - 1))):
+            sign = 0.25 if s == 0 else -0.25
+            beyond_v = ns_ref[s, 2 * EDGE + level : 2 * EDGE + level + 1]
+            source[level, outer : outer + 1] = source[level, outer : outer + 1] - sign * v_tall[level, inside : inside + 1]
+            source[level, inside : inside + 1] = source[level, inside : inside + 1] + sign * beyond_v
         full = (
-            source[level]
+            source[level, here]
             + jnp.where(lane == 0, 0.25 * from_west(side_u, level), 0.0)
             - jnp.where(lane == LANES - 1, 0.25 * from_east(side_u, level), 0.0)
         )
@@ -259,55 +258,77 @@
             )
         now, later = later, now
 
-    lane = lane_core
-    beyond = side[SWEEPS][core]
-    own = pad + HALO
+    side_ref[...] = side[SWEEPS][core]
+    for copy in copies:
+        copy.wait_send()
+
+
+def east_west_of(x, beyond, level, lane):
+    east = jnp.where(lane == LANES - 1, turn(beyond, LANES - 1 - 3 * EDGE - level * HALO), turn(x, -1))
+    west = jnp.where(lane == 0, turn(beyond, -(level * HALO + HALO - 1)), turn(x, 1))
+    return east, west
+
+
+def finish_kernel(
+    x_ref, side_ref, u_ref, v_tall, t_ref, p_ref,
+    zonal_hbm, meridional_hbm, theta_hbm, next_hbm, out, sem,
+):
+    levels, rows, _ = u_ref.shape
+    lane = lane_of(rows)
+    beyond = side_ref[...]
+    stores = []
     for level in range(levels):
-        x = now[level, own : own + rows]
-        next_ref[level] = x
-        zonal_ref[level] = u_ref[level] - 0.5 * gradient_weight * (east_of(x, beyond, level) - west_of(x, beyond, level))
-        north_south = now[level, own + 1 : own + 1 + rows] - now[level, own - 1 : own - 1 + rows]
-        meridional_ref[level] = v_ref[level] - 0.5 * gradient_weight * north_south
-        theta_ref[level] = t_ref[level] - adjust_weight * (x - p_ref[level])
+        x = x_ref[level, PAD : PAD + rows]
+        east, west = east_west_of(x, beyond, level, lane)
+        north_south = x_ref[level, PAD + 1 : PAD + 1 + rows] - x_ref[level, PAD - 1 : PAD - 1 + rows]
+        out[0, level] = u_ref[level] - 0.5 * gradient_weight * (east - west)
+        out[1, level] = v_tall[level, PAD : PAD + rows] - 0.5 * gradient_weight * north_south
+        out[2, level] = t_ref[level] - adjust_weight * (x - p_ref[level])
+        out[3, level] = x
+        if (level + 1) % CHUNK == 0:
+            done = pl.ds(level + 1 - CHUNK, CHUNK)
+            for i, hbm in enumerate((zonal_hbm, meridional_hbm, theta_hbm, next_hbm)):
+                store = pltpu.make_async_copy(out.at[i, done], hbm.at[done], sem.at[i, level // CHUNK])
+                store.start()
+                stores.append(store)
+    for store in stores:
+        store.wait()
 
 
 def on_device(nlon, nlat, *fields):
     levels, rows, columns = fields[0].shape
     assert (levels, columns) == (8, LANES)
     f32 = jnp.float32
-    vmem = pl.BlockSpec(memory_space=pltpu.VMEM)
     length = 2 * EDGE + levels + 2 * HALO
     high = rows + 2 * HALO
-    shapes = [(2, length, LANES), (2, rows, LANES), (2, 2, 2 * HALO, LANES), (2, rows, LANES)]
-    halos = pl.pallas_call(
-        functools.partial(halo_kernel, nlon, nlat),
-        out_shape=[jax.ShapeDtypeStruct(s, f32) for s in shapes],
-        in_specs=[vmem] * 5,
-        out_specs=[vmem] * 4,
+    block, padded = (levels, rows, LANES), (levels, rows + 2 * PAD, LANES)
+    kept = [padded, (rows, LANES), block, padded, block, block]
+    shapes = [
+        padded, (2, length, LANES), (2, rows, LANES), (2, 2, 2 * HALO, LANES), (2, rows, LANES), (2, length, LANES),
+        (4, high, LANES), padded, (6, levels, high, LANES), padded,
+    ]
+    held = pl.pallas_call(
+        functools.partial(kernel, nlon, nlat),
+        out_shape=[pltpu.VMEM(shape, f32) for shape in kept],
+        in_specs=[pl.BlockSpec(memory_space=pl.ANY)] * 5,
+        out_specs=[pl.BlockSpec(memory_space=pltpu.VMEM)] * 6,
+        scratch_shapes=[pltpu.VMEM(shape, f32) for shape in shapes]
+        + [pltpu.SemaphoreType.DMA((5,)), pltpu.SemaphoreType.DMA((8,)), pltpu.SemaphoreType.DMA((8,))],
+        compiler_params=pltpu.CompilerParams(collective_id=0, has_side_effects=True),
+        name="halo_step",
+    )(*fields)
+    held = [pltpu.with_memory_space_constraint(x, pltpu.VMEM) for x in held]
+    outputs = pl.pallas_call(
+        finish_kernel,
+        out_shape=[jax.ShapeDtypeStruct(block, f32)] * 4,
+        in_specs=[pl.BlockSpec(memory_space=pltpu.VMEM)] * 6,
+        out_specs=[pl.BlockSpec(memory_space=pl.ANY)] * 4,
         scratch_shapes=[
-            pltpu.VMEM((2, length, LANES), f32),
-            pltpu.SemaphoreType.DMA((8,)),
-            pltpu.SemaphoreType.DMA((8,)),
+            pltpu.VMEM((4, levels, rows, LANES), f32),
+            pltpu.SemaphoreType.DMA((4, levels // CHUNK)),
         ],
-        compiler_params=pltpu.CompilerParams(collective_id=0, has_side_effects=True),
-        name="halo",
-    )(*fields)
-    outputs = pl.pallas_call(
-        step_kernel,
-        out_shape=[jax.ShapeDtypeStruct((levels, rows, LANES), f32)] * 4,
-        in_specs=[vmem] * 9,
-        out_specs=[vmem] * 4,
-        scratch_shapes=[
-            pltpu.VMEM((4, high, LANES), f32),
-            pltpu.VMEM((high, LANES), f32),
-            pltpu.VMEM((levels, high + 16, LANES), f32),
-            pltpu.VMEM((levels, high, LANES), f32),
-            pltpu.VMEM((6, levels, high, LANES), f32),
-            pltpu.VMEM((levels, high + 16, LANES), f32),
-            pltpu.VMEM((levels, high + 16, LANES), f32),
-        ],
-        name="step",
-    )(*fields, *halos)
+        name="finish",
+    )(*held)
     return tuple(outputs)
 
 

time: 15.6 us -> 13.1 us (0.84)
  Pallas kernels: 14.8 us -> 12.3 us
    pallas_call x2, Pallas kernels: 14.8 us -> 12.3 us  [the longest x1 11.3 us: on_device(): pl.pallas_call(functools.partial(kernel, nlon, nlat), out_shape=[pltpu.VM...]
where the time goes in v2:
time: 13.1 us; the launch traced here: 13 us
  Pallas kernels  12.3 us (94%)
  between operations  0.64 us (5%)
    pallas_call x1, Pallas kernels, on_device(): pl.pallas_call(functools.partial(kernel, nlon, nlat), out_shape=[pltpu.VM...  11.3 us
    pallas_call x1, Pallas kernels, on_device(): pl.pallas_call(finish_kernel, out_shape=[jax.ShapeDtypeStruct(block, f32)...  1.02 us

profile of v2, /device:TPU:0, one launch (start us, length us, event | category | flops | bytes accessed | tf_op | source)
XLA Modules:
  0.0 13.0 jit_solution(17626317949338074281)
XLA Ops:
  0.6 11.3 %halo_step.1 = (f32[8,48,128]{2,1,0:T(8,128)S(1)}, f32[32,128]{1,0:T(8,128)S(1)}, f32[8,32,128]{2,1,0:T(8,128)S(1)}, f32[8,48,128]{2,1,0:T(8,128)S(1)}, f32[8,32...) custom-call(f32[8,32,128]{2,1,0:T(8,128)} %u_hbm.1, f32[8,32,128]{2,1,0:T(8,128)} %v_hbm.1, f32[8,32,128]{2,1,0:T(8,128)} %t_hbm.1, ...), custom_call_target="tpu_custom_call" | custom-call | tf_op jit(solution)/shard_map/halo_step/pallas_call | solution.py:310
  12.0 1.0 %finish.1 = (f32[8,32,128]{2,1,0:T(8,128)}, f32[8,32,128]{2,1,0:T(8,128)}, f32[8,32,128]{2,1,0:T(8,128)}, f32[8,32,128]{2,1,0:T(8,128)}) custom-call(f32[8,48,128]{2,1,0:T(8,128)S(1)} %get-tuple-element.10.x_ref, f32[32,128]{1,0:T(8,128)S(1)} %get-tuple-element.11.side_ref, f32[8,32,128]{2,1,0:T(8,128)S(1)} %get-tuple-element.12.u_ref, ...), custom_call_target="tpu_custom_call" | custom-call | tf_op jit(solution)/shard_map/finish/pallas_call | solution.py:321

commit v3 on v2

--- a/solution.py
+++ b/solution.py
@@ -9,7 +9,7 @@
 
 SWEEPS = 3
 HALO = SWEEPS + 1
-CHUNK = 2
+CHUNK = 4
 LANES = 128
 PAD = 8
 EDGE = 8 * HALO
@@ -35,7 +35,7 @@
     nlon, nlat, u_hbm, v_hbm, t_hbm, p_hbm, k_hbm,
     xb, side_ref, u_ref, v_tall, t_ref, p_ref,
     k_tall, ns_ref, ew_ref, cn_ref, own_ref, ns_send,
-    tall, source, coef, xa, load_sem, send_sem, recv_sem,
+    tall, coef, xa, load_sem, send_sem, recv_sem,
 ):
     levels, rows, _ = t_ref.shape
     lon, lat = lax.axis_index("lon"), lax.axis_index("lat")
@@ -81,19 +81,12 @@
         u_diff = jnp.where(lane == LANES - 1, 0.0, turn(u, -1)) - jnp.where(lane == 0, 0.0, turn(u, 1))
         v_diff = jnp.where(row_id == rows - 1, 0.0, turn(v, -1, 0)) - jnp.where(row_id == 0, 0.0, turn(v, 1, 0))
         part = p_ref[level] - 0.5 * divergence_weight * (u_diff + v_diff) + thermal_weight * t_ref[level]
-        source[level, inner] = part
+        xa[level, inner] = part
         for index, field in enumerate((part, k, u, v)):
             slot = index * levels + level
             moved = turn(field, (slot + 1) * HALO)
             east = jnp.where(group == slot, moved, east)
             west = jnp.where(group == (slot + 1) % (LANES // HALO), moved, west)
-        for s in (0, 1):
-            for r in range(HALO):
-                here = slice(first[s] + r, first[s] + r + 1)
-                ns_send[s, pl.ds(level * HALO + place[s][r], 1)] = part[here]
-                ns_send[s, pl.ds(EDGE + level * HALO + place[s][r], 1)] = k[here]
-            edge = slice(0, 1) if s == 0 else slice(rows - 1, rows)
-            ns_send[s, 2 * EDGE + level : 2 * EDGE + level + 1] = v[edge] * signs[s]
     west = turn(west, -HALO)
     own_ref[0] = west
     own_ref[1] = east
@@ -122,24 +115,55 @@
             device_id=beside(1), device_id_type=MESH,
         ).wait_recv()
 
-    for s in (0, 1):
-        there = jnp.where(poles[s], s, 1 - s)
-        send(ns_send.at[s], ns_ref.at[there], partner(s, 0), 2 + s, 2 + there)
-        corner = ns_send.at[s, pl.ds(base, 2 * HALO)]
-        send(corner, cn_ref.at[there, 1], partner(s, -1), 4 + 2 * s, 4 + 2 * there + 1)
-        send(corner, cn_ref.at[there, 0], partner(s, 1), 5 + 2 * s, 4 + 2 * there)
     send(own_ref.at[0], ew_ref.at[1], beside(-1), 0, 1)
     send(own_ref.at[1], ew_ref.at[0], beside(1), 1, 0)
+    there = [jnp.where(poles[s], s, 1 - s) for s in (0, 1)]
+    for s in (0, 1):
+        corner = ns_send.at[s, pl.ds(base, 2 * HALO)]
+        send(corner, cn_ref.at[there[s], 1], partner(s, -1), 4 + 2 * s, 4 + 2 * there[s] + 1)
+        send(corner, cn_ref.at[there[s], 0], partner(s, 1), 5 + 2 * s, 4 + 2 * there[s])
+    for s in (0, 1):
+        for level in range(levels):
+            for r in range(HALO):
+                here = slice(PAD + first[s] + r, PAD + first[s] + r + 1)
+                ns_send[s, pl.ds(level * HALO + place[s][r], 1)] = xa[level, here]
+                ns_send[s, pl.ds(EDGE + level * HALO + place[s][r], 1)] = k_tall[level, here]
+            edge = PAD if s == 0 else PAD + rows - 1
+            ns_send[s, 2 * EDGE + level : 2 * EDGE + level + 1] = v_tall[level, edge : edge + 1] * signs[s]
+        send(ns_send.at[s], ns_ref.at[there[s]], partner(s, 0), 2 + s, 2 + there[s])
+
+    high = rows + 2 * HALO
+    core = slice(HALO, HALO + rows)
+    top = HALO + rows
+    bottom = PAD - HALO
+    zero_row = jnp.zeros((1, LANES), jnp.float32)
+
+    def weigh(level, start, count):
+        at = lambda shift: slice(start + shift, start + shift + count)
+        k = k_tall[level, at(0)]
+        ke = 0.5 * (k + turn(k, -1))
+        kw = 0.5 * (k + turn(k, 1))
+        kn = 0.5 * (k + k_tall[level, at(1)])
+        ks = 0.5 * (k + k_tall[level, at(-1)])
+        vertical = vertical_coupling * ((level > 0) + (level < levels - 1))
+        inv = 1.0 / (1.0 + ke + kw + kn + ks + vertical)
+        found = (xa[level, at(0)] * inv, ke * inv, kw * inv, kn * inv, ks * inv, vertical_coupling * inv)
+        for index, value in enumerate(found):
+            coef[index, level, at(0)] = value
+
+    for level in range(levels):
+        for ref in (xa, xb, k_tall):
+            ref[level, bottom - 1 : bottom] = zero_row
+            ref[level, bottom + high : bottom + high + 1] = zero_row
+        for start in (bottom, PAD + rows):
+            k_tall[level, start : start + HALO] = jnp.zeros((HALO, LANES), jnp.float32)
+        weigh(level, PAD, rows)
+
     for side in (0, 1):
         arrive(ew_ref.at[side], side)
         arrive(ns_ref.at[side], 2 + side)
         arrive(cn_ref.at[side, 0], 4 + 2 * side)
         arrive(cn_ref.at[side, 1], 5 + 2 * side)
-
-    high = rows + 2 * HALO
-    core = slice(HALO, HALO + rows)
-    top = HALO + rows
-    bottom = PAD - HALO
 
     tall[0, core], tall[1, core] = ew_ref[0], own_ref[0]
     tall[2, core], tall[3, core] = own_ref[1], ew_ref[1]
@@ -194,52 +218,29 @@
             + up * turn(x, -HALO) + down * turn(x, HALO)
         )
 
-    def from_west(x, level):
-        return turn(x, -(level * HALO + HALO - 1))
-
-    def from_east(x, level):
-        return turn(x, LANES - 1 - 3 * EDGE - level * HALO)
-
-    def east_of(x, beyond, level):
-        return jnp.where(lane == LANES - 1, from_east(beyond, level), turn(x, -1))
-
-    def west_of(x, beyond, level):
-        return jnp.where(lane == 0, from_west(beyond, level), turn(x, 1))
+    rims = [jnp.where(column == HALO - 1, turn(x, -(EDGE + HALO)), x) for x in side]
+    edge = (lane == 0) | (lane == LANES - 1)
+
+    def with_edges(x, step, level):
+        return jnp.where(edge, turn(rims[step], -(EDGE + level * HALO)), x)
 
     here = slice(bottom, bottom + high)
     north, south = slice(bottom + 1, bottom + 1 + high), slice(bottom - 1, bottom - 1 + high)
-    zero_row = jnp.zeros((1, LANES), jnp.float32)
     for level in range(levels):
-        for ref in (xa, xb, k_tall):
-            ref[level, bottom - 1 : bottom] = zero_row
-            ref[level, bottom + high : bottom + high + 1] = zero_row
         for s, start in ((0, bottom), (1, PAD + rows)):
-            source[level, start : start + HALO] = ns_ref[s, level * HALO : (level + 1) * HALO]
+            xa[level, start : start + HALO] = ns_ref[s, level * HALO : (level + 1) * HALO]
             k_tall[level, start : start + HALO] = ns_ref[s, EDGE + level * HALO : EDGE + (level + 1) * HALO]
         for s, (outer, inside) in enumerate(((PAD - 1, PAD), (PAD + rows, PAD + rows - 1))):
             sign = 0.25 if s == 0 else -0.25
             beyond_v = ns_ref[s, 2 * EDGE + level : 2 * EDGE + level + 1]
-            source[level, outer : outer + 1] = source[level, outer : outer + 1] - sign * v_tall[level, inside : inside + 1]
-            source[level, inside : inside + 1] = source[level, inside : inside + 1] + sign * beyond_v
-        full = (
-            source[level, here]
-            + jnp.where(lane == 0, 0.25 * from_west(side_u, level), 0.0)
-            - jnp.where(lane == LANES - 1, 0.25 * from_east(side_u, level), 0.0)
-        )
-        k = k_tall[level, here]
-        ke = 0.5 * (k + east_of(k, side_k, level))
-        kw = 0.5 * (k + west_of(k, side_k, level))
-        kn = 0.5 * (k + k_tall[level, north])
-        ks = 0.5 * (k + k_tall[level, south])
-        count = vertical_coupling * ((level > 0) + (level < levels - 1))
-        inv = 1.0 / (1.0 + ke + kw + kn + ks + count)
-        xa[level, here] = full
-        for index, value in enumerate((full * inv, ke * inv, kw * inv, kn * inv, ks * inv, vertical_coupling * inv)):
-            coef[index, level] = value
+            xa[level, outer : outer + 1] = xa[level, outer : outer + 1] - sign * v_tall[level, inside : inside + 1]
+            xa[level, inside : inside + 1] = xa[level, inside : inside + 1] + sign * beyond_v
+        for start in (bottom, PAD + rows - HALO):
+            weigh(level, start, 2 * HALO)
+        xa[level, here] = with_edges(xa[level, here], 0, level)
 
     now, later = xa, xb
     for sweep in range(SWEEPS):
-        beyond = side[sweep]
         for level in range(levels):
             x = now[level, here]
             if level == 0:
@@ -248,14 +249,15 @@
                 column_sum = now[level - 1, here]
             else:
                 column_sum = now[level + 1, here] + now[level - 1, here]
-            later[level, here] = (
-                coef[0, level]
-                + coef[1, level] * east_of(x, beyond, level)
-                + coef[2, level] * west_of(x, beyond, level)
-                + coef[3, level] * now[level, north]
-                + coef[4, level] * now[level, south]
-                + coef[5, level] * column_sum
+            value = (
+                coef[0, level, here]
+                + coef[1, level, here] * turn(x, -1)
+                + coef[2, level, here] * turn(x, 1)
+                + coef[3, level, here] * now[level, north]
+                + coef[4, level, here] * now[level, south]
+                + coef[5, level, here] * column_sum
             )
+            later[level, here] = with_edges(value, sweep + 1, level)
         now, later = later, now
 
     side_ref[...] = side[SWEEPS][core]
@@ -276,7 +278,8 @@
     levels, rows, _ = u_ref.shape
     lane = lane_of(rows)
     beyond = side_ref[...]
-    stores = []
+    stores = [pltpu.make_async_copy(x_ref.at[:, pl.ds(PAD, rows)], next_hbm, sem.at[3, 0])]
+    stores[0].start()
     for level in range(levels):
         x = x_ref[level, PAD : PAD + rows]
         east, west = east_west_of(x, beyond, level, lane)
@@ -284,10 +287,9 @@
         out[0, level] = u_ref[level] - 0.5 * gradient_weight * (east - west)
         out[1, level] = v_tall[level, PAD : PAD + rows] - 0.5 * gradient_weight * north_south
         out[2, level] = t_ref[level] - adjust_weight * (x - p_ref[level])
-        out[3, level] = x
         if (level + 1) % CHUNK == 0:
             done = pl.ds(level + 1 - CHUNK, CHUNK)
-            for i, hbm in enumerate((zonal_hbm, meridional_hbm, theta_hbm, next_hbm)):
+            for i, hbm in enumerate((zonal_hbm, meridional_hbm, theta_hbm)):
                 store = pltpu.make_async_copy(out.at[i, done], hbm.at[done], sem.at[i, level // CHUNK])
                 store.start()
                 stores.append(store)
@@ -305,7 +307,7 @@
     kept = [padded, (rows, LANES), block, padded, block, block]
     shapes = [
         padded, (2, length, LANES), (2, rows, LANES), (2, 2, 2 * HALO, LANES), (2, rows, LANES), (2, length, LANES),
-        (4, high, LANES), padded, (6, levels, high, LANES), padded,
+        (4, high, LANES), (6, levels, rows + 2 * PAD, LANES), padded,
     ]
     held = pl.pallas_call(
         functools.partial(kernel, nlon, nlat),
@@ -324,7 +326,7 @@
         in_specs=[pl.BlockSpec(memory_space=pltpu.VMEM)] * 6,
         out_specs=[pl.BlockSpec(memory_space=pl.ANY)] * 4,
         scratch_shapes=[
-            pltpu.VMEM((4, levels, rows, LANES), f32),
+            pltpu.VMEM((3, levels, rows, LANES), f32),
             pltpu.SemaphoreType.DMA((4, levels // CHUNK)),
         ],
         name="finish",

time: 13.1 us -> 12.6 us (0.962)
  the two profiles are of different devices: /device:TPU:0 before, /device:TPU:1 now
where the time goes in v3:
time: 12.6 us; the launch traced here: 12.4 us
  Pallas kernels  11.8 us (94%)
  between operations  0.64 us (5%)
    pallas_call x1, Pallas kernels, on_device(): pl.pallas_call(functools.partial(kernel, nlon, nlat), out_shape=[pltpu.VM...  10.8 us
    pallas_call x1, Pallas kernels, on_device(): pl.pallas_call(finish_kernel, out_shape=[jax.ShapeDtypeStruct(block, f32)...  0.95 us

profile of v3, /device:TPU:1, one launch (start us, length us, event | category | flops | bytes accessed | tf_op | source)
XLA Modules:
  0.0 12.4 jit_solution(3533744718802764188)
XLA Ops:
  0.6 10.8 %halo_step.1 = (f32[8,48,128]{2,1,0:T(8,128)S(1)}, f32[32,128]{1,0:T(8,128)S(1)}, f32[8,32,128]{2,1,0:T(8,128)S(1)}, f32[8,48,128]{2,1,0:T(8,128)S(1)}, f32[8,32...) custom-call(f32[8,32,128]{2,1,0:T(8,128)} %u_hbm.1, f32[8,32,128]{2,1,0:T(8,128)} %v_hbm.1, f32[8,32,128]{2,1,0:T(8,128)} %t_hbm.1, ...), custom_call_target="tpu_custom_call" | custom-call | tf_op jit(solution)/shard_map/halo_step/pallas_call | solution.py:312
  11.5 0.9 %finish.1 = (f32[8,32,128]{2,1,0:T(8,128)}, f32[8,32,128]{2,1,0:T(8,128)}, f32[8,32,128]{2,1,0:T(8,128)}, f32[8,32,128]{2,1,0:T(8,128)}) custom-call(f32[8,48,128]{2,1,0:T(8,128)S(1)} %get-tuple-element.10.x_ref, f32[32,128]{1,0:T(8,128)S(1)} %get-tuple-element.11.side_ref, f32[8,32,128]{2,1,0:T(8,128)S(1)} %get-tuple-element.12.u_ref, ...), custom_call_target="tpu_custom_call" | custom-call | tf_op jit(solution)/shard_map/finish/pallas_call | solution.py:323

commit v4 on v3

--- a/solution.py
+++ b/solution.py
@@ -59,14 +59,12 @@
     loads = [
         pltpu.make_async_copy(src, dst, load_sem.at[i])
         for i, (src, dst) in enumerate((
-            (u_hbm, u_ref), (v_hbm, v_tall.at[:, pl.ds(PAD, rows)]), (t_hbm, t_ref),
-            (p_hbm, p_ref), (k_hbm, k_tall.at[:, pl.ds(PAD, rows)]),
+            (k_hbm, k_tall.at[:, pl.ds(PAD, rows)]), (u_hbm, u_ref),
+            (v_hbm, v_tall.at[:, pl.ds(PAD, rows)]), (t_hbm, t_ref), (p_hbm, p_ref),
         ))
     ]
     for load in loads:
         load.start()
-    for load in loads:
-        load.wait()
     inner = slice(PAD, PAD + rows)
     lane = lane_of(rows)
     group = lane // HALO
@@ -76,17 +74,31 @@
     signs = [jnp.where(poles[s], -1.0, 1.0).astype(jnp.float32) for s in (0, 1)]
     west = jnp.zeros((rows, LANES), jnp.float32)
     east = jnp.zeros((rows, LANES), jnp.float32)
-    for level in range(levels):
-        u, v, k = u_ref[level], v_tall[level, inner], k_tall[level, inner]
+
+    def packed(pair, field, index, level):
+        slot = index * levels + level
+        moved = turn(field, (slot + 1) * HALO)
+        west, east = pair
+        return (
+            jnp.where(group == (slot + 1) % (LANES // HALO), moved, west),
+            jnp.where(group == slot, moved, east),
+        )
+
+    pair = (west, east)
+    for index, ref, load in ((1, k_tall, loads[0]), (2, u_ref, loads[1]), (3, v_tall, loads[2])):
+        load.wait()
+        for level in range(levels):
+            pair = packed(pair, ref[level] if ref is u_ref else ref[level, inner], index, level)
+    loads[3].wait()
+    loads[4].wait()
+    for level in range(levels):
+        u, v = u_ref[level], v_tall[level, inner]
         u_diff = jnp.where(lane == LANES - 1, 0.0, turn(u, -1)) - jnp.where(lane == 0, 0.0, turn(u, 1))
         v_diff = jnp.where(row_id == rows - 1, 0.0, turn(v, -1, 0)) - jnp.where(row_id == 0, 0.0, turn(v, 1, 0))
         part = p_ref[level] - 0.5 * divergence_weight * (u_diff + v_diff) + thermal_weight * t_ref[level]
         xa[level, inner] = part
-        for index, field in enumerate((part, k, u, v)):
-            slot = index * levels + level
-            moved = turn(field, (slot + 1) * HALO)
-            east = jnp.where(group == slot, moved, east)
-            west = jnp.where(group == (slot + 1) % (LANES // HALO), moved, west)
+        pair = packed(pair, part, 0, level)
+    west, east = pair
     west = turn(west, -HALO)
     own_ref[0] = west
     own_ref[1] = east
@@ -160,8 +172,20 @@
         weigh(level, PAD, rows)
 
     for side in (0, 1):
+        arrive(ns_ref.at[side], 2 + side)
+    for level in range(levels):
+        for s, start in ((0, bottom), (1, PAD + rows)):
+            xa[level, start : start + HALO] = ns_ref[s, level * HALO : (level + 1) * HALO]
+            k_tall[level, start : start + HALO] = ns_ref[s, EDGE + level * HALO : EDGE + (level + 1) * HALO]
+        for s, (outer, inside) in enumerate(((PAD - 1, PAD), (PAD + rows, PAD + rows - 1))):
+            sign = 0.25 if s == 0 else -0.25
+            beyond_v = ns_ref[s, 2 * EDGE + level : 2 * EDGE + level + 1]
+            xa[level, outer : outer + 1] = xa[level, outer : outer + 1] - sign * v_tall[level, inside : inside + 1]
+            xa[level, inside : inside + 1] = xa[level, inside : inside + 1] + sign * beyond_v
+        for start in (bottom, PAD + rows - HALO):
+            weigh(level, start, 2 * HALO)
+    for side in (0, 1):
         arrive(ew_ref.at[side], side)
-        arrive(ns_ref.at[side], 2 + side)
         arrive(cn_ref.at[side, 0], 4 + 2 * side)
         arrive(cn_ref.at[side, 1], 5 + 2 * side)
 
@@ -227,16 +251,6 @@
     here = slice(bottom, bottom + high)
     north, south = slice(bottom + 1, bottom + 1 + high), slice(bottom - 1, bottom - 1 + high)
     for level in range(levels):
-        for s, start in ((0, bottom), (1, PAD + rows)):
-            xa[level, start : start + HALO] = ns_ref[s, level * HALO : (level + 1) * HALO]
-            k_tall[level, start : start + HALO] = ns_ref[s, EDGE + level * HALO : EDGE + (level + 1) * HALO]
-        for s, (outer, inside) in enumerate(((PAD - 1, PAD), (PAD + rows, PAD + rows - 1))):
-            sign = 0.25 if s == 0 else -0.25
-            beyond_v = ns_ref[s, 2 * EDGE + level : 2 * EDGE + level + 1]
-            xa[level, outer : outer + 1] = xa[level, outer : outer + 1] - sign * v_tall[level, inside : inside + 1]
-            xa[level, inside : inside + 1] = xa[level, inside : inside + 1] + sign * beyond_v
-        for start in (bottom, PAD + rows - HALO):
-            weigh(level, start, 2 * HALO)
         xa[level, here] = with_edges(xa[level, here], 0, level)
 
     now, later = xa, xb

time: 12.6 us -> 12.4 us (0.984)
  the two profiles are of different devices: /device:TPU:1 before, /device:TPU:0 now
where the time goes in v4:
time: 12.4 us; the launch traced here: 12.2 us
  Pallas kernels  11.6 us (94%)
  between operations  0.64 us (5%)
    pallas_call x1, Pallas kernels, on_device(): pl.pallas_call(functools.partial(kernel, nlon, nlat), out_shape=[pltpu.VM...  10.6 us
    pallas_call x1, Pallas kernels, on_device(): pl.pallas_call(finish_kernel, out_shape=[jax.ShapeDtypeStruct(block, f32)...  0.95 us

profile of v4, /device:TPU:0, one launch (start us, length us, event | category | flops | bytes accessed | tf_op | source)
XLA Modules:
  0.0 12.2 jit_solution(15328628898636569209)
XLA Ops:
  0.6 10.6 %halo_step.1 = (f32[8,48,128]{2,1,0:T(8,128)S(1)}, f32[32,128]{1,0:T(8,128)S(1)}, f32[8,32,128]{2,1,0:T(8,128)S(1)}, f32[8,48,128]{2,1,0:T(8,128)S(1)}, f32[8,32...) custom-call(f32[8,32,128]{2,1,0:T(8,128)} %u_hbm.1, f32[8,32,128]{2,1,0:T(8,128)} %v_hbm.1, f32[8,32,128]{2,1,0:T(8,128)} %t_hbm.1, ...), custom_call_target="tpu_custom_call" | custom-call | tf_op jit(solution)/shard_map/halo_step/pallas_call | solution.py:326
  11.3 0.9 %finish.1 = (f32[8,32,128]{2,1,0:T(8,128)}, f32[8,32,128]{2,1,0:T(8,128)}, f32[8,32,128]{2,1,0:T(8,128)}, f32[8,32,128]{2,1,0:T(8,128)}) custom-call(f32[8,48,128]{2,1,0:T(8,128)S(1)} %get-tuple-element.10.x_ref, f32[32,128]{1,0:T(8,128)S(1)} %get-tuple-element.11.side_ref, f32[8,32,128]{2,1,0:T(8,128)S(1)} %get-tuple-element.12.u_ref, ...), custom_call_target="tpu_custom_call" | custom-call | tf_op jit(solution)/shard_map/finish/pallas_call | solution.py:337

commit v5 on v4

--- a/solution.py
+++ b/solution.py
@@ -110,6 +110,14 @@
             ns_send[s, pl.ds(base + place[s][r], 1)] = west[here] * flip
             ns_send[s, pl.ds(base + HALO + place[s][r], 1)] = east[here] * flip
 
+    for s in (0, 1):
+        for level in range(levels):
+            for r in range(HALO):
+                here = slice(PAD + first[s] + r, PAD + first[s] + r + 1)
+                ns_send[s, pl.ds(level * HALO + place[s][r], 1)] = xa[level, here]
+                ns_send[s, pl.ds(EDGE + level * HALO + place[s][r], 1)] = k_tall[level, here]
+            edge = PAD if s == 0 else PAD + rows - 1
+            ns_send[s, 2 * EDGE + level : 2 * EDGE + level + 1] = v_tall[level, edge : edge + 1] * signs[s]
     pl.semaphore_wait(barrier, len(everyone))
     copies = []
 
@@ -131,18 +139,11 @@
     send(own_ref.at[1], ew_ref.at[0], beside(1), 1, 0)
     there = [jnp.where(poles[s], s, 1 - s) for s in (0, 1)]
     for s in (0, 1):
+        send(ns_send.at[s], ns_ref.at[there[s]], partner(s, 0), 2 + s, 2 + there[s])
+    for s in (0, 1):
         corner = ns_send.at[s, pl.ds(base, 2 * HALO)]
         send(corner, cn_ref.at[there[s], 1], partner(s, -1), 4 + 2 * s, 4 + 2 * there[s] + 1)
         send(corner, cn_ref.at[there[s], 0], partner(s, 1), 5 + 2 * s, 4 + 2 * there[s])
-    for s in (0, 1):
-        for level in range(levels):
-            for r in range(HALO):
-                here = slice(PAD + first[s] + r, PAD + first[s] + r + 1)
-                ns_send[s, pl.ds(level * HALO + place[s][r], 1)] = xa[level, here]
-                ns_send[s, pl.ds(EDGE + level * HALO + place[s][r], 1)] = k_tall[level, here]
-            edge = PAD if s == 0 else PAD + rows - 1
-            ns_send[s, 2 * EDGE + level : 2 * EDGE + level + 1] = v_tall[level, edge : edge + 1] * signs[s]
-        send(ns_send.at[s], ns_ref.at[there[s]], partner(s, 0), 2 + s, 2 + there[s])
 
     high = rows + 2 * HALO
     core = slice(HALO, HALO + rows)

time: 12.4 us -> 12.4 us (level)
  the two profiles are of different devices: /device:TPU:0 before, /device:TPU:1 now
where the time goes in v5:
time: 12.4 us; the launch traced here: 12.3 us
  Pallas kernels  11.7 us (94%)
  between operations  0.64 us (5%)
    pallas_call x1, Pallas kernels, on_device(): pl.pallas_call(functools.partial(kernel, nlon, nlat), out_shape=[pltpu.VM...  10.7 us
    pallas_call x1, Pallas kernels, on_device(): pl.pallas_call(finish_kernel, out_shape=[jax.ShapeDtypeStruct(block, f32)...  0.95 us

profile of v5, /device:TPU:1, one launch (start us, length us, event | category | flops | bytes accessed | tf_op | source)
XLA Modules:
  0.0 12.3 jit_solution(3593790367150717133)
XLA Ops:
  0.6 10.7 %halo_step.1 = (f32[8,48,128]{2,1,0:T(8,128)S(1)}, f32[32,128]{1,0:T(8,128)S(1)}, f32[8,32,128]{2,1,0:T(8,128)S(1)}, f32[8,48,128]{2,1,0:T(8,128)S(1)}, f32[8,32...) custom-call(f32[8,32,128]{2,1,0:T(8,128)} %u_hbm.1, f32[8,32,128]{2,1,0:T(8,128)} %v_hbm.1, f32[8,32,128]{2,1,0:T(8,128)} %t_hbm.1, ...), custom_call_target="tpu_custom_call" | custom-call | tf_op jit(solution)/shard_map/halo_step/pallas_call | solution.py:327
  11.3 0.9 %finish.1 = (f32[8,32,128]{2,1,0:T(8,128)}, f32[8,32,128]{2,1,0:T(8,128)}, f32[8,32,128]{2,1,0:T(8,128)}, f32[8,32,128]{2,1,0:T(8,128)}) custom-call(f32[8,48,128]{2,1,0:T(8,128)S(1)} %get-tuple-element.10.x_ref, f32[32,128]{1,0:T(8,128)S(1)} %get-tuple-element.11.side_ref, f32[8,32,128]{2,1,0:T(8,128)S(1)} %get-tuple-element.12.u_ref, ...), custom_call_target="tpu_custom_call" | custom-call | tf_op jit(solution)/shard_map/finish/pallas_call | solution.py:338
